TPU v7x, 32 devices: a whole 2x2x4 slice. The times are simulated.
32 devices in a mesh: groups: 2 (over x), dom: 16 (over z, y, core).
Axes of the slice: x: 2, y: 2, z: 4, core: 2. Of those that a mesh axis runs over, the one named last changes fastest.
Arguments:
- source: bfloat16 [72, 262144], P(None, ('groups', 'dom')), parts along dimension 1, may hold values from -6 to 6
- tile_weight: bfloat16 [8192, 128, 128], P('dom'), may hold values from -0.0625 to 0.0625
- tile_source: int32 [8192], P('dom'), may hold values from 0 to 127
- tile_slot: int32 [8192], P('dom'), may hold values from 0 to 15
- tile_count: int32 [16], P('dom'), may hold values from 64 to 512, as said below
- dest_block: int32 [256], P('dom'), may hold values from 0 to 63, as said below
- embed_weight: bfloat16 [1152, 1024], replicated, may hold values from -0.1875 to 0.1875
- embed_bias: float32 [1024], replicated, may hold values from -3 to 3
Outputs:
- remapped: bfloat16 [128, 72, 128], P(('groups', 'dom')), parts along dimension 0
- embedded: bfloat16 [1024, 1024], P(('groups', 'dom')), parts along dimension 0
There are 2 independent parts, one for each index of `groups`. A program takes and returns all parts, laid end to end along the dimension named above; an argument that names none is the same for every part. Nothing has to cross between parts.
Inputs may be any that keep to these rules, and one draw needn't show every extreme that they name: `tile_count`: number of live tiles of each device; the later tile slots are unused. Some device has all 512 tiles live. `dest_block`: the owner of target block b is device b // 4. Within one device's 16 entries the blocks are distinct and at most 2 of them belong to any one owner; on every device some owner has exactly 2.
All inputs are finite; a program needn't handle non-finite values.
Results may differ from a plain program's by a relative error of at most 0.0046.
Values may be sent and summed in bfloat16 or wider, within the bound.
A program may use at most 128 MiB of HBM per device.

v0:
```python
import jax
import jax.numpy as jnp
from jax import lax
from jax.sharding import PartitionSpec as P

PATCH = 4
CAP = 2
TB_DEV = 4


def extended_2(cells, sides, width):
    for axis, dim in sides:
        count = lax.axis_size(axis)
        head = lax.slice_in_dim(cells, 0, width, axis=dim)
        tail = lax.slice_in_dim(cells, cells.shape[dim] - width, cells.shape[dim], axis=dim)
        cells = jnp.concatenate(
            [
                lax.ppermute(tail, axis, [(i, (i + 1) % count) for i in range(count)]),
                cells,
                lax.ppermute(head, axis, [((i + 1) % count, i) for i in range(count)]),
            ],
            axis=dim,
        )
    return cells


def local(
    source, tile_weight, tile_source, tile_slot, tile_count, dest_block, embed_weight, embed_bias
):
    channels, own_cells = source.shape
    block_size = tile_weight.shape[1]
    own_blocks = own_cells // block_size
    rim_blocks = own_blocks // 2
    ext_count = own_blocks + 2 * rim_blocks
    tile_total = tile_weight.shape[0]
    slot_total = dest_block.shape[0]
    group_size = 128
    extended = extended_2(source, (("dom", 1),), rim_blocks * block_size)
    ext_blocks = extended.reshape(channels, ext_count, block_size)
    live_total = tile_count[0]
    slot_ids = jnp.arange(slot_total, dtype=jnp.int32)
    block_ids = jnp.arange(ext_count, dtype=jnp.int32)

    def add_group(group, totals):
        first = group * group_size
        indices = lax.dynamic_slice_in_dim(tile_source, first, group_size)
        choose = (indices[:, None] == block_ids[None, :]).astype(jnp.bfloat16)
        picked = jnp.einsum(
            "gb,cbi->cgi", choose, ext_blocks, preferred_element_type=jnp.float32
        ).astype(jnp.bfloat16)
        weights = lax.dynamic_slice_in_dim(tile_weight, first, group_size, 0)
        products = jnp.einsum("cgi,gij->gcj", picked, weights, preferred_element_type=jnp.float32)
        active = first + jnp.arange(group_size, dtype=jnp.int32) < live_total
        targets = lax.dynamic_slice_in_dim(tile_slot, first, group_size)
        placing = ((slot_ids[:, None] == targets[None, :]) & active[None, :]).astype(jnp.float32)
        return totals + jnp.einsum(
            "sg,gcj->scj", placing, products, precision=lax.Precision.HIGHEST
        )

    group_count = tile_total // group_size
    combined = lax.fori_loop(
        0, group_count, add_group, jnp.zeros((slot_total, channels, block_size), jnp.float32)
    )
    peers = lax.axis_size("dom")
    owners = dest_block // TB_DEV
    local_rows = dest_block % TB_DEV
    earlier = (owners[None, :] == owners[:, None]) & (slot_ids[None, :] < slot_ids[:, None])
    position = owners * CAP + jnp.sum(earlier.astype(jnp.int32), axis=1)
    buffer_rows = jnp.arange(peers * CAP, dtype=jnp.int32)
    placing = position[None, :] == buffer_rows[:, None]
    outgoing = jnp.einsum(
        "bs,scj->bcj", placing.astype(jnp.float32), combined, precision=lax.Precision.HIGHEST
    )
    labels = jnp.sum(jnp.where(placing, local_rows[None, :] + 1, 0), axis=1) - 1
    incoming, arrived = (
        lax.all_to_all(outgoing, "dom", split_axis=0, concat_axis=0, tiled=True),
        lax.all_to_all(labels, "dom", split_axis=0, concat_axis=0, tiled=True),
    )
    owned_rows = jnp.arange(TB_DEV, dtype=jnp.int32)
    collect = (arrived[None, :] == owned_rows[:, None]).astype(jnp.float32)
    summed = jnp.einsum("kb,bcj->kcj", collect, incoming, precision=lax.Precision.HIGHEST)
    remapped = summed.astype(jnp.bfloat16)
    per_block = block_size // (PATCH * PATCH)
    patches = remapped.reshape(TB_DEV, channels, PATCH, per_block, PATCH)
    patches = patches.transpose(0, 3, 1, 2, 4).reshape(TB_DEV * per_block, channels * PATCH * PATCH)
    embedded = jnp.dot(patches, embed_weight, preferred_element_type=jnp.float32) + embed_bias
    return (remapped, embedded.astype(jnp.bfloat16))


def solution(mesh):
    placed = (
        P(None, ("groups", "dom")),
        P("dom", None, None),
        P("dom"),
        P("dom"),
        P("dom"),
        P("dom"),
        P(),
        P(),
    )
    return jax.shard_map(
        local,
        mesh=mesh,
        in_specs=placed,
        out_specs=(P(("groups", "dom"), None, None), P(("groups", "dom"), None)),
        check_vma=False,
    )
```

profile of v0, /device:TPU:15, one launch (start us, length us, event | category | flops | bytes accessed | tf_op | source)
XLA Modules:
  0.0 132.9 jit_solution(14130334814147793098)
XLA Ops:
  0.6 0.0 copy-start
  0.6 0.0 copy-start.3
  0.7 2.5 %fusion.36 = (bf16[72,4096]{1,0:T(8,128)(2,1)}, bf16[72,4096]{1,0:T(8,128)(2,1)}) fusion(bf16[72,8192]{1,0:T(8,128)(2,1)} %param.10), kind=kLoop, calls=%fused_computation.44 | loop fusion | bytes 2359296 | tf_op jit(solution)/shard_map/slice | solution.py:15
  3.2 0.7 collective-permute-start.1
  3.8 2.0 %collective-permute-start = (bf16[72,4096]{1,0:T(8,128)(2,1)}, bf16[72,4096]{1,0:T(8,128)(2,1)}, u32[]{:S(2)}, u32[]{:S(2)}) collective-permute-start(bf16[72,4096]{1,0:T(8,128)(2,1)} %get-tuple-element.207), channel_id=1, source_target_pairs={{0,1},{1,2},{2,3},{3,4},{4,5},{5,6},{6,7},{7,8},{8,9},{9,10},{10,1... | collective-permute-start | bytes 1769480 | tf_op jit(solution)/shard_map/ppermute | solution.py:18
  5.8 0.0 copy-done.3
  5.8 0.2 convert_reduce_fusion
  6.0 0.1 select_reduce_fusion
  6.1 0.7 sub.12
  6.8 7.8 %all-to-all-start = ((s32[16,2,1]{1,2,0:T(1,128)}), s32[16,2,1]{1,2,0:T(1,128)S(1)}, u32[]{:S(2)}, u32[]{:S(2)}) async-start(s32[16,2,1]{1,2,0:T(1,128)} %bitcast), calls=%async_computation | async-start | bytes 16384 | tf_op jit(solution)/shard_map/all_to_all | solution.py:77
  14.6 0.0 collective-permute-done.1
  14.6 0.0 collective-permute-done
  14.6 1.6 %maximum_bitcast_fusion = bf16[9,8,128,128]{3,1,2,0:T(8,128)(2,1)S(1)} fusion(bf16[72,4096]{1,0:T(8,128)(2,1)S(1)} %collective-permute-done.1, bf16[72,8192]{1,0:T(8,128)(2,1)} %param.10, bf16[72,4096]{1,0:T(8,128)(2,1)} %collective-permute-done), kind=kLoop, calls=%fused_computation.19 | loop fusion | flops 7077888 | bytes 4718592
  16.2 2.1 %copy.30 = bf16[9,8,128,128]{3,2,1,0:T(8,128)(2,1)} copy(bf16[9,8,128,128]{3,1,2,0:T(8,128)(2,1)S(1)} %maximum_bitcast_fusion) | data formatting | bytes 4718592
  18.3 63.4 %while.14 = (s32[]{:T(128)}, f32[16,72,128]{2,0,1:T(8,128)S(1)}, s32[512]{0:T(512)}, s32[]{:T(128)}, s32[512]{0:T(512)}, /*index=5*/bf16[72,128,128]{2,1,0:T(8,1...) while((s32[]{:T(128)}, f32[16,72,128]{2,0,1:T(8,128)S(1)}, ...), condition=%wide.region_3.4_spmd.clone, body=%wide.region_2.3_spmd.clone.sunk | while | flops 831967488 | bytes 21892544 | solution.py:61
  18.3 0.8 dynamic_slice.30
  19.1 2.5 %convert_bitcast_fusion.2 = bf16[72,128,128]{2,1,0:T(8,128)(2,1)S(1)} fusion(bf16[72,128,128]{2,1,0:T(8,128)(2,1)} %get-tuple-element.281, s32[128]{0:T(128)S(1)} %dynamic_slice.30), kind=kOutput, calls=%fused_computation.7.clone.1 | convolution fusion | flops 303185920 | bytes 4719104 | tf_op jit(solution)/shard_map/while/body/eval_jaxpr/gb,cbi->cgi/dot_general | solution.py:48
  21.6 6.9 %fusion.55 = f32[128,72,128]{2,1,0:T(8,128)} fusion(bf16[512,128,128]{2,1,0:T(8,128)(2,1)} %get-tuple-element.282, s32[]{:T(128)S(6)} %select_n.35, bf16[72,128,128]{2,1,0:T(8,128)(2,1)S(1)} %convert_bitcast_fusion.2), kind=kOutput, calls=%fused_computation.4.clone.1 | convolution fusion | flops 301989888 | bytes 11272196 | tf_op jit(solution)/shard_map/while/body/eval_jaxpr/cgi,gij->gcj/dot_general | solution.py:52
  28.4 0.8 dynamic_slice.31
  29.2 0.7 add_compare_fusion.2
  29.9 4.3 %fusion.56 = f32[16,72,128]{2,0,1:T(8,128)S(1)} fusion(f32[128,72,128]{2,1,0:T(8,128)} %fusion.55, f32[16,72,128]{2,0,1:T(8,128)S(1)} %get-tuple-element.266, pred[]{:T(512)S(6)} %compare.6, s32[128]{0:T(128)S(1)} %dynamic_slice.31, pred[128]{0:T(512)(128)(4,1)S(1)} %add_compare_fusion.2), kind=kOutput, calls=%fused_computation.8.clone.1 | convolution fusion | flops 226791424 | bytes 5898881 | tf_op jit(solution)/shard_map/while/body/eval_jaxpr/sg,gcj->scj/dot_general | solution.py:56
  34.2 0.8 dynamic_slice.30
  34.9 2.5 %convert_bitcast_fusion.2 = bf16[72,128,128]{2,1,0:T(8,128)(2,1)S(1)} fusion(bf16[72,128,128]{2,1,0:T(8,128)(2,1)} %get-tuple-element.281, s32[128]{0:T(128)S(1)} %dynamic_slice.30), kind=kOutput, calls=%fused_computation.7.clone.1 | convolution fusion | flops 303185920 | bytes 4719104 | tf_op jit(solution)/shard_map/while/body/eval_jaxpr/gb,cbi->cgi/dot_general | solution.py:48
  37.4 6.9 %fusion.55 = f32[128,72,128]{2,1,0:T(8,128)} fusion(bf16[512,128,128]{2,1,0:T(8,128)(2,1)} %get-tuple-element.282, s32[]{:T(128)S(6)} %select_n.35, bf16[72,128,128]{2,1,0:T(8,128)(2,1)S(1)} %convert_bitcast_fusion.2), kind=kOutput, calls=%fused_computation.4.clone.1 | convolution fusion | flops 301989888 | bytes 11272196 | tf_op jit(solution)/shard_map/while/body/eval_jaxpr/cgi,gij->gcj/dot_general | solution.py:52
  44.3 0.8 dynamic_slice.31
  45.1 0.7 add_compare_fusion.2
  45.7 4.3 %fusion.56 = f32[16,72,128]{2,0,1:T(8,128)S(1)} fusion(f32[128,72,128]{2,1,0:T(8,128)} %fusion.55, f32[16,72,128]{2,0,1:T(8,128)S(1)} %get-tuple-element.266, pred[]{:T(512)S(6)} %compare.6, s32[128]{0:T(128)S(1)} %dynamic_slice.31, pred[128]{0:T(512)(128)(4,1)S(1)} %add_compare_fusion.2), kind=kOutput, calls=%fused_computation.8.clone.1 | convolution fusion | flops 226791424 | bytes 5898881 | tf_op jit(solution)/shard_map/while/body/eval_jaxpr/sg,gcj->scj/dot_general | solution.py:56
  50.0 0.8 dynamic_slice.30
  50.8 2.5 %convert_bitcast_fusion.2 = bf16[72,128,128]{2,1,0:T(8,128)(2,1)S(1)} fusion(bf16[72,128,128]{2,1,0:T(8,128)(2,1)} %get-tuple-element.281, s32[128]{0:T(128)S(1)} %dynamic_slice.30), kind=kOutput, calls=%fused_computation.7.clone.1 | convolution fusion | flops 303185920 | bytes 4719104 | tf_op jit(solution)/shard_map/while/body/eval_jaxpr/gb,cbi->cgi/dot_general | solution.py:48
  53.3 6.9 %fusion.55 = f32[128,72,128]{2,1,0:T(8,128)} fusion(bf16[512,128,128]{2,1,0:T(8,128)(2,1)} %get-tuple-element.282, s32[]{:T(128)S(6)} %select_n.35, bf16[72,128,128]{2,1,0:T(8,128)(2,1)S(1)} %convert_bitcast_fusion.2), kind=kOutput, calls=%fused_computation.4.clone.1 | convolution fusion | flops 301989888 | bytes 11272196 | tf_op jit(solution)/shard_map/while/body/eval_jaxpr/cgi,gij->gcj/dot_general | solution.py:52
  60.2 0.8 dynamic_slice.31
  60.9 0.7 add_compare_fusion.2
  61.6 4.3 %fusion.56 = f32[16,72,128]{2,0,1:T(8,128)S(1)} fusion(f32[128,72,128]{2,1,0:T(8,128)} %fusion.55, f32[16,72,128]{2,0,1:T(8,128)S(1)} %get-tuple-element.266, pred[]{:T(512)S(6)} %compare.6, s32[128]{0:T(128)S(1)} %dynamic_slice.31, pred[128]{0:T(512)(128)(4,1)S(1)} %add_compare_fusion.2), kind=kOutput, calls=%fused_computation.8.clone.1 | convolution fusion | flops 226791424 | bytes 5898881 | tf_op jit(solution)/shard_map/while/body/eval_jaxpr/sg,gcj->scj/dot_general | solution.py:56
  65.9 0.8 dynamic_slice.30
  66.7 2.5 %convert_bitcast_fusion.2 = bf16[72,128,128]{2,1,0:T(8,128)(2,1)S(1)} fusion(bf16[72,128,128]{2,1,0:T(8,128)(2,1)} %get-tuple-element.281, s32[128]{0:T(128)S(1)} %dynamic_slice.30), kind=kOutput, calls=%fused_computation.7.clone.1 | convolution fusion | flops 303185920 | bytes 4719104 | tf_op jit(solution)/shard_map/while/body/eval_jaxpr/gb,cbi->cgi/dot_general | solution.py:48
  69.1 6.9 %fusion.55 = f32[128,72,128]{2,1,0:T(8,128)} fusion(bf16[512,128,128]{2,1,0:T(8,128)(2,1)} %get-tuple-element.282, s32[]{:T(128)S(6)} %select_n.35, bf16[72,128,128]{2,1,0:T(8,128)(2,1)S(1)} %convert_bitcast_fusion.2), kind=kOutput, calls=%fused_computation.4.clone.1 | convolution fusion | flops 301989888 | bytes 11272196 | tf_op jit(solution)/shard_map/while/body/eval_jaxpr/cgi,gij->gcj/dot_general | solution.py:52
  76.0 0.8 dynamic_slice.31
  76.8 0.7 add_compare_fusion.2
  77.4 4.3 %fusion.56 = f32[16,72,128]{2,0,1:T(8,128)S(1)} fusion(f32[128,72,128]{2,1,0:T(8,128)} %fusion.55, f32[16,72,128]{2,0,1:T(8,128)S(1)} %get-tuple-element.266, pred[]{:T(512)S(6)} %compare.6, s32[128]{0:T(128)S(1)} %dynamic_slice.31, pred[128]{0:T(512)(128)(4,1)S(1)} %add_compare_fusion.2), kind=kOutput, calls=%fused_computation.8.clone.1 | convolution fusion | flops 226791424 | bytes 5898881 | tf_op jit(solution)/shard_map/while/body/eval_jaxpr/sg,gcj->scj/dot_general | solution.py:56
  81.7 0.7 fusion.29
  82.5 1.7 %copy.25 = f32[32,72,128]{2,1,0:T(8,128)} copy(f32[32,72,128]{2,0,1:T(8,128)S(1)} %fusion.29) | data formatting | bytes 2359296 | tf_op jit(solution)/shard_map/bs,scj->bcj/dot_general | solution.py:71
  84.2 0.0 all-to-all-done
  84.2 11.1 %all-to-all-start.1 = ((f32[32,72,128]{2,1,0:T(8,128)}), f32[32,72,128]{2,1,0:T(8,128)S(1)}, u32[]{:S(2)}, u32[]{:S(2)}) async-start(f32[32,72,128]{2,1,0:T(8,128)} %copy.25), calls=%async_computation.1 | async-start | bytes 2359296 | tf_op jit(solution)/shard_map/all_to_all | solution.py:76
  95.3 0.5 broadcast.79
  95.8 0.7 reduce.3
  96.5 0.0 copy-start.2
  96.5 0.1 eq.115
  96.6 26.5 %all-to-all-done.1 = f32[32,72,128]{2,1,0:T(8,128)S(1)} async-done(((f32[32,72,128]{2,1,0:T(8,128)}), f32[32,72,128]{2,1,0:T(8,128)S(1)}, u32[]{:S(2)}, u32[]{:S(2)}) %all-to-all-start.1) | async-done | bytes 1179680 | tf_op jit(solution)/shard_map/all_to_all | solution.py:76
  123.1 0.6 fusion.23
  123.7 0.0 copy-start.1
  123.7 0.6 copy-done.1
  124.3 0.6 copy.29
  124.9 1.6 %copy.27 = bf16[4,72,128]{1,2,0:T(8,128)(2,1)} copy(bf16[4,72,128]{2,0,1:T(4,128)(2,1)} %copy-done.1) | data formatting | bytes 147456 | tf_op jit(solution)/shard_map/convert_element_type | solution.py:82
  126.6 2.9 %copy.28 = bf16[4,8,72,4,4]{1,0,4,3,2:T(4,128)(2,1)S(1)} copy(bf16[4,8,72,4,4]{2,4,1,3,0:T(4,128)(2,1)} %bitcast.38) | data formatting | bytes 147456 | tf_op jit(solution)/shard_map/transpose | solution.py:85
  129.5 1.3 reshape.46
  130.8 0.0 copy-done
  130.8 0.0 copy-done.2
  130.8 2.1 %fusion.26 = bf16[32,1024]{1,0:T(8,128)(2,1)} fusion(bf16[32,1152]{0,1:T(8,128)(2,1)} %reshape.46, bf16[1152,1024]{1,0:T(8,128)(2,1)S(1)} %copy-done, f32[1024]{0:T(1024)S(1)} %copy-done.2), kind=kOutput, calls=%fused_computation.24 | convolution fusion | flops 75563008 | bytes 2502656 | tf_op jit(solution)/shard_map/dot_general | solution.py:86
  (4 shorter events, 0.0 us)
Async XLA Ops:
  0.6 130.2 %copy-start = (bf16[1152,1024]{1,0:T(8,128)(2,1)S(1)}, bf16[1152,1024]{1,0:T(8,128)(2,1)}, u32[]{:S(2)}) copy-start(bf16[1152,1024]{1,0:T(8,128)(2,1)} %param.16) | copy-start | bytes 7077892
  0.6 5.2 %copy-start.3 = (s32[16]{0:T(128)S(1)}, s32[16]{0:T(128)}, u32[]{:S(2)}) copy-start(s32[16]{0:T(128)} %param.15) | copy-start | bytes 196
  3.2 11.4 %collective-permute-start.1 = (bf16[72,4096]{1,0:T(8,128)(2,1)}, bf16[72,4096]{1,0:T(8,128)(2,1)S(1)}, u32[]{:S(2)}, u32[]{:S(2)}) collective-permute-start(bf16[72,4096]{1,0:T(8,128)(2,1)} %get-tuple-element.208), channel_id=1, source_target_pairs={{1,0},{2,1},{3,2},{4,3},{5,4},{6,5},{7,6},{8,7},{9,8},{10,9},{11,1... | collective-permute-start | bytes 1769480 | tf_op jit(solution)/shard_map/ppermute | solution.py:20
  3.8 10.8 %collective-permute-start = (bf16[72,4096]{1,0:T(8,128)(2,1)}, bf16[72,4096]{1,0:T(8,128)(2,1)}, u32[]{:S(2)}, u32[]{:S(2)}) collective-permute-start(bf16[72,4096]{1,0:T(8,128)(2,1)} %get-tuple-element.207), channel_id=1, source_target_pairs={{0,1},{1,2},{2,3},{3,4},{4,5},{5,6},{6,7},{7,8},{8,9},{9,10},{10,1... | collective-permute-start | bytes 1769480 | tf_op jit(solution)/shard_map/ppermute | solution.py:18
  6.8 77.4 %all-to-all-start = ((s32[16,2,1]{1,2,0:T(1,128)}), s32[16,2,1]{1,2,0:T(1,128)S(1)}, u32[]{:S(2)}, u32[]{:S(2)}) async-start(s32[16,2,1]{1,2,0:T(1,128)} %bitcast), calls=%async_computation | async-start | bytes 16384 | tf_op jit(solution)/shard_map/all_to_all | solution.py:77
  84.2 38.9 %all-to-all-start.1 = ((f32[32,72,128]{2,1,0:T(8,128)}), f32[32,72,128]{2,1,0:T(8,128)S(1)}, u32[]{:S(2)}, u32[]{:S(2)}) async-start(f32[32,72,128]{2,1,0:T(8,128)} %copy.25), calls=%async_computation.1 | async-start | bytes 2359296 | tf_op jit(solution)/shard_map/all_to_all | solution.py:76
  96.5 34.3 %copy-start.2 = (f32[1024]{0:T(1024)S(1)}, f32[1024]{0:T(1024)}, u32[]{:S(2)}) copy-start(f32[1024]{0:T(1024)} %param.17) | copy-start | bytes 12292
  123.7 0.6 copy-start.1
where the time goes:
time: 134 us; the launch traced here: 133 us
  matrix products  58.1 us (43%)
  waiting for transfers between devices  26.5 us (20%)
  starting transfers between devices  21.6 us (16%)
  local copies, waits for them, and re-layouts  20.8 us (16%)
  other arithmetic  5.14 us (4%)
    dot_general x4, matrix products, add_group(): jnp.einsum('cgi,gij->gcj', picked, weights, preferred_element_type=jnp.fl...  27.6 us
    all_to_all x1, waiting for transfers between devices, local(): lax.all_to_all(outgoing, 'dom', split_axis=0, concat_axis=0, tiled=True)  26.5 us
    dot_general x4, matrix products, add_group(): jnp.einsum('sg,gcj->scj', placing, products, precision=lax.Precision.HIGH...  17.2 us
    all_to_all x1, starting transfers between devices, local(): lax.all_to_all(outgoing, 'dom', split_axis=0, concat_axis=0, tiled=True)  11.1 us
    dot_general x4, matrix products, add_group(): jnp.einsum('gb,cbi->cgi', choose, ext_blocks, preferred_element_type=jnp....  9.92 us
    all_to_all x1, starting transfers between devices, local(): lax.all_to_all(labels, 'dom', split_axis=0, concat_axis=0, tiled=True)  7.79 us
    unnamed x10, local copies, waits for them, and re-layouts  3.39 us
    dynamic_slice x4, local copies, waits for them, and re-layouts, add_group(): indices = lax.dynamic_slice_in_dim(tile_source, first, group_size)  3.03 us
  transfers between devices with their start and end apart: 4, of which 1 were waited for; matrix products, arithmetic and copies ran while one was open for 54% of the time, Pallas kernels for 0%

commit v1 on v0

v1 whole, which is shorter than its diff:
```python
import functools

import jax
import jax.numpy as jnp
from jax import lax
from jax.experimental import pallas as pl
from jax.experimental.pallas import tpu as pltpu
from jax.sharding import PartitionSpec as P

PATCH = 4
CAP = 2
TB_DEV = 4
GROUP = 16
DEPTH = 4


def tile_steps(order_ref, count_ref, weight_ref, cells_ref, acc_ref, buffer, sems):
    groups = (count_ref[0] + GROUP - 1) // GROUP

    def fetch(group):
        slot = lax.rem(group, DEPTH)
        for i in range(GROUP):
            tile = order_ref[group * GROUP + i] & 0xFFF
            pltpu.make_async_copy(
                weight_ref.at[tile], buffer.at[slot, i], sems.at[slot]
            ).start()

    for group in range(DEPTH):
        @pl.when(group < groups)
        def _():
            fetch(group)

    def step(group, _):
        slot = lax.rem(group, DEPTH)
        pltpu.make_async_copy(
            weight_ref.at[pl.ds(0, GROUP)], buffer.at[slot], sems.at[slot]
        ).wait()
        for first in range(0, GROUP, 4):
            rows, products = [], []
            for i in range(first, first + 4):
                code = order_ref[group * GROUP + i]
                block = (code >> 12) & 0xFF
                rows.append(code >> 20)
                cells = cells_ref[:, pl.ds(pl.multiple_of(block * 128, 128), 128)]
                products.append(
                    jnp.dot(cells, buffer[slot, i], preferred_element_type=jnp.float32)
                )
            for row, product in zip(rows, products):
                acc_ref[row] += product

        @pl.when(group + DEPTH < groups)
        def _():
            fetch(group + DEPTH)

        return 0

    lax.fori_loop(0, groups, step, 0)


def near_kernel(
    order_ref, count_ref, weight_ref, own_ref, fast_ref, acc_ref, cells, buffer, sems, cell_sem
):
    own_cells = own_ref.shape[1]
    copies = [
        pltpu.make_async_copy(own_ref, cells.at[:, pl.ds(0, own_cells)], cell_sem.at[0]),
        pltpu.make_async_copy(
            fast_ref, cells.at[:, pl.ds(own_cells, fast_ref.shape[1])], cell_sem.at[1]
        ),
    ]
    for copy in copies:
        copy.start()
    acc_ref[...] = jnp.zeros_like(acc_ref)
    for copy in copies:
        copy.wait()
    tile_steps(order_ref, count_ref, weight_ref, cells, acc_ref, buffer, sems)


def far_kernel(
    order_ref, count_ref, weight_ref, slow_ref, acc_in_ref, out_ref, acc, buffer, sems, acc_sem
):
    copy = pltpu.make_async_copy(acc_in_ref, acc, acc_sem)
    copy.start()
    copy.wait()
    tile_steps(order_ref, count_ref, weight_ref, slow_ref, acc, buffer, sems)
    rows = out_ref.shape[0]
    out_ref[...] = acc[pl.ds(0, rows)].astype(jnp.bfloat16)


def exchange_kernel(
    peers,
    out_ref,
    label_ref,
    embed_ref,
    bias_ref,
    remapped_ref,
    embedded_ref,
    incoming,
    labels,
    embed,
    padded,
    turned,
    send_sem,
    recv_sem,
    label_send_sem,
    label_recv_sem,
    embed_sem,
):
    me = lax.axis_index("dom")
    channels = out_ref.shape[2]
    barrier = pltpu.get_barrier_semaphore()

    def greet(k, _):
        pl.semaphore_signal(
            barrier,
            inc=1,
            device_id={"dom": lax.rem(me + k, peers)},
            device_id_type=pl.DeviceIdType.MESH,
        )
        return 0

    lax.fori_loop(1, peers, greet, 0)
    embed_copy = pltpu.make_async_copy(embed_ref, embed, embed_sem)
    embed_copy.start()
    pl.semaphore_wait(barrier, peers - 1)

    def copies(k):
        peer = lax.rem(me + k, peers)
        return (
            pltpu.make_async_remote_copy(
                src_ref=label_ref.at[peer],
                dst_ref=labels.at[me],
                send_sem=label_send_sem.at[k],
                recv_sem=label_recv_sem.at[k],
                device_id={"dom": peer},
                device_id_type=pl.DeviceIdType.MESH,
            ),
            pltpu.make_async_remote_copy(
                src_ref=out_ref.at[peer],
                dst_ref=incoming.at[me],
                send_sem=send_sem.at[k],
                recv_sem=recv_sem.at[k],
                device_id={"dom": peer},
                device_id_type=pl.DeviceIdType.MESH,
            ),
        )

    def send(k, _):
        for copy in copies(k):
            copy.start()
        return 0

    lax.fori_loop(1, peers, send, 0)

    def add(totals, rows, names):
        totals = list(totals)
        for r in range(CAP):
            row = rows[r].astype(jnp.float32)
            name = jnp.broadcast_to(names[r : r + 1, :], row.shape)
            for b in range(TB_DEV):
                totals[b] = totals[b] + jnp.where(name == float(b), row, 0.0)
        return tuple(totals)

    zero = jnp.zeros((channels, 128), jnp.float32)
    totals = add((zero,) * TB_DEV, out_ref[me], label_ref[me])

    def receive(k, totals):
        for copy in copies(k):
            copy.wait_recv()
        source = lax.rem(me - k + peers, peers)
        return add(totals, incoming[source], labels[source])

    totals = lax.fori_loop(1, peers, receive, totals)
    padded[...] = jnp.zeros_like(padded)
    for b in range(TB_DEV):
        rounded = totals[b].astype(jnp.bfloat16)
        remapped_ref[b] = rounded
        padded[b, pl.ds(0, channels), :] = rounded.astype(jnp.float32)
    for b in range(TB_DEV):
        turned[pl.ds(b * 128, 128), :] = padded[b].T
    embed_copy.wait()
    per_block = 128 // (PATCH * PATCH)
    stride = PATCH * per_block
    result = jnp.zeros(embedded_ref.shape, jnp.float32)
    for r in range(PATCH):
        for q in range(PATCH):
            parts = [
                turned[pl.ds(b * 128 + r * stride + q, per_block, stride=PATCH), :]
                for b in range(TB_DEV)
            ]
            patch = jnp.concatenate(parts, axis=0).astype(jnp.bfloat16)[:, :channels]
            result = result + jnp.dot(
                patch, embed[r * PATCH + q], preferred_element_type=jnp.float32
            )
    embedded_ref[...] = (result + bias_ref[...]).astype(jnp.bfloat16)

    def finish(k, _):
        for copy in copies(k):
            copy.wait_send()
        return 0

    lax.fori_loop(1, peers, finish, 0)


def local(
    peers,
    source,
    tile_weight,
    tile_source,
    tile_slot,
    tile_count,
    dest_block,
    embed_weight,
    embed_bias,
):
    channels, own_cells = source.shape
    block_size = tile_weight.shape[1]
    own_blocks = own_cells // block_size
    rim_blocks = own_blocks // 2
    rim = rim_blocks * block_size
    tile_total = tile_weight.shape[0]
    slot_total = dest_block.shape[0]
    emb = embed_weight.shape[1]
    rows_out = peers * CAP
    me = lax.axis_index("dom")
    odd = me % 2
    head_start, tail_start = 0, own_cells - rim
    slow_part = lax.dynamic_slice_in_dim(source, jnp.where(odd == 1, tail_start, head_start), rim, 1)
    fast_part = lax.dynamic_slice_in_dim(source, jnp.where(odd == 1, head_start, tail_start), rim, 1)
    slow_pairs = [(i, (i + 1) % peers if i % 2 else (i - 1) % peers) for i in range(peers)]
    fast_pairs = [(i, i + 1 - 2 * (i % 2)) for i in range(peers)]
    fast = lax.ppermute(fast_part, "dom", fast_pairs)
    slow = lax.ppermute(slow_part, "dom", slow_pairs)

    slot_ids = jnp.arange(slot_total, dtype=jnp.int32)
    owners = dest_block // TB_DEV
    earlier = (owners[None, :] == owners[:, None]) & (slot_ids[None, :] < slot_ids[:, None])
    position = owners * CAP + jnp.sum(earlier.astype(jnp.int32), axis=1)
    out_rows = jnp.arange(rows_out, dtype=jnp.int32)
    named = jnp.sum(
        jnp.where(position[None, :] == out_rows[:, None], dest_block[None, :] % TB_DEV + 1, 0), axis=1
    ) - 1
    names = jnp.broadcast_to(
        jnp.pad(named.reshape(peers, CAP), ((0, 0), (0, 8 - CAP)))[:, :, None], (peers, 8, 128)
    ).astype(jnp.float32)

    tile_ids = jnp.arange(tile_total, dtype=jnp.int32)
    row_of = jnp.sum(
        jnp.where(tile_slot[:, None] == slot_ids[None, :], position[None, :], 0), axis=1
    )
    live = tile_ids < tile_count[0]
    left = tile_source < rim_blocks
    right = tile_source >= rim_blocks + own_blocks
    is_far = jnp.where(odd == 1, right, left)
    near = live & ~is_far
    far = live & is_far
    near_block = jnp.where(
        left,
        tile_source + own_blocks,
        jnp.where(right, tile_source - rim_blocks, tile_source - rim_blocks),
    )
    far_block = jnp.where(left, tile_source, tile_source - rim_blocks - own_blocks)
    block = jnp.where(is_far, far_block, near_block)
    code = tile_ids | (block << 12) | (row_of << 20)
    pad_code = rows_out << 20

    def listed(chosen):
        rank = jnp.sum(
            (chosen[None, :] & (tile_ids[None, :] < tile_ids[:, None])).astype(jnp.int32), axis=1
        )
        hit = chosen[None, :] & (rank[None, :] == tile_ids[:, None])
        order = jnp.sum(jnp.where(hit, code[None, :] - pad_code, 0), axis=1) + pad_code
        return order, jnp.sum(chosen.astype(jnp.int32)).reshape(1)

    near_order, near_count = listed(near)
    far_order, far_count = listed(far)

    smem = pl.BlockSpec(memory_space=pltpu.SMEM)
    vmem = pl.BlockSpec(memory_space=pltpu.VMEM)
    hbm = pl.BlockSpec(memory_space=pl.ANY)
    acc_shape = (rows_out + 1, channels, block_size)
    ring = [
        pltpu.VMEM((DEPTH, GROUP, block_size, block_size), jnp.bfloat16),
        pltpu.SemaphoreType.DMA((DEPTH,)),
    ]
    partial = pl.pallas_call(
        near_kernel,
        out_shape=jax.ShapeDtypeStruct(acc_shape, jnp.float32),
        in_specs=[smem, smem, hbm, hbm, hbm],
        out_specs=vmem,
        scratch_shapes=[
            pltpu.VMEM((channels, own_cells + rim), jnp.bfloat16),
            *ring,
            pltpu.SemaphoreType.DMA((2,)),
        ],
        compiler_params=pltpu.CompilerParams(vmem_limit_bytes=32 * 2**20),
        cost_estimate=pl.CostEstimate(
            flops=2 * tile_total * channels * block_size**2,
            bytes_accessed=tile_weight.size * 2,
            transcendentals=0,
        ),
        name="near_tiles",
    )(near_order, near_count, tile_weight, source, fast)
    outgoing = pl.pallas_call(
        far_kernel,
        out_shape=jax.ShapeDtypeStruct((rows_out, channels, block_size), jnp.bfloat16),
        in_specs=[smem, smem, hbm, vmem, hbm],
        out_specs=vmem,
        scratch_shapes=[
            pltpu.VMEM(acc_shape, jnp.float32),
            *ring,
            pltpu.SemaphoreType.DMA,
        ],
        compiler_params=pltpu.CompilerParams(vmem_limit_bytes=32 * 2**20),
        cost_estimate=pl.CostEstimate(
            flops=tile_total * channels * block_size**2,
            bytes_accessed=tile_weight.size,
            transcendentals=0,
        ),
        name="far_tiles",
    )(far_order, far_count, tile_weight, slow, partial)

    per_patch = PATCH * PATCH
    embed_turned = embed_weight.reshape(channels, per_patch, emb).transpose(1, 0, 2)
    patch_rows = TB_DEV * (block_size // per_patch)
    remapped, embedded = pl.pallas_call(
        functools.partial(exchange_kernel, peers),
        out_shape=(
            jax.ShapeDtypeStruct((TB_DEV, channels, block_size), jnp.bfloat16),
            jax.ShapeDtypeStruct((patch_rows, emb), jnp.bfloat16),
        ),
        in_specs=[vmem, vmem, hbm, vmem],
        out_specs=(vmem, vmem),
        scratch_shapes=[
            pltpu.VMEM((peers, CAP, channels, block_size), jnp.bfloat16),
            pltpu.VMEM((peers, 8, 128), jnp.float32),
            pltpu.VMEM((per_patch, channels, emb), jnp.bfloat16),
            pltpu.VMEM((TB_DEV, 128, 128), jnp.float32),
            pltpu.VMEM((TB_DEV * 128, 128), jnp.float32),
            pltpu.SemaphoreType.DMA((peers,)),
            pltpu.SemaphoreType.DMA((peers,)),
            pltpu.SemaphoreType.DMA((peers,)),
            pltpu.SemaphoreType.DMA((peers,)),
            pltpu.SemaphoreType.DMA,
        ],
        compiler_params=pltpu.CompilerParams(
            collective_id=0, has_side_effects=True, vmem_limit_bytes=32 * 2**20
        ),
        name="exchange",
    )(
        outgoing.reshape(peers, CAP, channels, block_size),
        names,
        embed_turned,
        embed_bias.reshape(1, emb),
    )
    return remapped, embedded


def solution(mesh):
    placed = (
        P(None, ("groups", "dom")),
        P("dom", None, None),
        P("dom"),
        P("dom"),
        P("dom"),
        P("dom"),
        P(),
        P(),
    )
    return jax.shard_map(
        functools.partial(local, mesh.shape["dom"]),
        mesh=mesh,
        in_specs=placed,
        out_specs=(P(("groups", "dom"), None, None), P(("groups", "dom"), None)),
        check_vma=False,
    )
```

time: 134 us -> 84.5 us (0.63); the launches traced: 133 us -> 85.2 us
  Pallas kernels: 0 us -> 60.4 us
  matrix products: 58.1 us -> 0 us
  waiting for transfers between devices: 26.5 us -> 0.01 us
  starting transfers between devices: 21.6 us -> 1.8 us
  local copies, waits for them, and re-layouts: 20.8 us -> 17.9 us
  other arithmetic: 5.14 us -> 3.64 us
    pallas_call x0 -> x3, Pallas kernels: none -> 60.4 us  [the longest x1 47.5 us: local(): pl.pallas_call(functools.partial(exchange_kernel, peers), out_shape=(jax....]
    dot_general x15 -> x0, matrix products: 58.1 us -> none  [the longest x4 27.6 us: add_group(): jnp.einsum('cgi,gij->gcj', picked, weights, preferred_element_type=jnp.fl...]
    all_to_all x2 -> x0, waiting for transfers between devices: 26.5 us -> none  [the longest x1 26.5 us: local(): lax.all_to_all(outgoing, 'dom', split_axis=0, concat_axis=0, tiled=True)]
    all_to_all x2 -> x0, starting transfers between devices: 18.9 us -> none  [the longest x1 11.1 us: local(): lax.all_to_all(outgoing, 'dom', split_axis=0, concat_axis=0, tiled=True)]
    unnamed x10 -> x24, local copies, waits for them, and re-layouts: 3.39 us -> 13.4 us
    dynamic_slice x8 -> x1, local copies, waits for them, and re-layouts: 6.05 us -> 2.51 us  [local(): lax.dynamic_slice_in_dim(source, jnp.where(odd == 1, head_start, tail_sta...]
    transpose x1 -> x0, local copies, waits for them, and re-layouts: 2.9 us -> none  [local(): patches.transpose(0, 3, 1, 2, 4)]
    reduce_sum x1 -> x7, other arithmetic: 0.09 us -> 2.9 us  [the longest x2 1.33 us: listed(): return (order, jnp.sum(chosen.astype(jnp.int32)).reshape(1))]
  transfers between devices with their start and end apart: 4 -> 2, of which waited for: 1 -> 0; matrix products, arithmetic and copies ran while one was open for 54% -> 7% of each run, Pallas kernels for 0% -> 9%
where the time goes in v1:
time: 84.5 us; the launch traced here: 85.2 us
  Pallas kernels  60.4 us (71%)
  local copies, waits for them, and re-layouts  17.9 us (21%)
  other arithmetic  3.64 us (4%)
  starting transfers between devices  1.8 us (2%)
  between operations  1.49 us (2%)
    pallas_call x1, Pallas kernels, local(): pl.pallas_call(functools.partial(exchange_kernel, peers), out_shape=(jax....  47.5 us
    unnamed x24, local copies, waits for them, and re-layouts  13.4 us
    pallas_call x1, Pallas kernels, local(): pl.pallas_call(near_kernel, out_shape=jax.ShapeDtypeStruct(acc_shape, jnp...  7.99 us
    pallas_call x1, Pallas kernels, local(): pl.pallas_call(far_kernel, out_shape=jax.ShapeDtypeStruct((rows_out, chan...  4.85 us
    dynamic_slice x1, local copies, waits for them, and re-layouts, local(): lax.dynamic_slice_in_dim(source, jnp.where(odd == 1, head_start, tail_sta...  2.51 us
  transfers between devices with their start and end apart: 2, of which 0 were waited for; matrix products, arithmetic and copies ran while one was open for 7% of the time, Pallas kernels for 9%

profile of v1, /device:TPU:15, one launch (start us, length us, event | category | flops | bytes accessed | tf_op | source)
XLA Modules:
  0.0 85.2 jit_solution(4576343816243712989)
XLA Ops:
  0.6 0.0 copy-start.10
  0.6 0.0 copy-start.8
  0.7 0.0 copy-start.5
  0.7 0.0 copy-start.4
  0.7 2.5 %constant_dynamic-slice_fusion = (bf16[72,4096]{1,0:T(8,128)(2,1)}, bf16[72,4096]{1,0:T(8,128)(2,1)}) fusion(bf16[72,8192]{1,0:T(8,128)(2,1)} %own_ref.1, s32[]{:T(128)S(6)} %select_n.73, s32[]{:T(128)S(6)} %select_n.71), kind=kLoop, calls=%fused_computation.41 | loop fusion | bytes 2359304 | tf_op jit(solution)/shard_map/dynamic_slice | solution.py:228
  3.2 0.7 collective-permute-start.1
  3.9 1.1 %collective-permute-start = (bf16[72,4096]{1,0:T(8,128)(2,1)}, bf16[72,4096]{1,0:T(8,128)(2,1)S(1)}, u32[]{:S(2)}, u32[]{:S(2)}) collective-permute-start(bf16[72,4096]{1,0:T(8,128)(2,1)} %get-tuple-element.10), channel_id=1, source_target_pairs={{0,15},{1,2},{2,1},{3,4},{4,3},{5,6},{6,5},{7,8},{8,7},{9,10},{10,... | collective-permute-start | bytes 1769480 | tf_op jit(solution)/shard_map/ppermute | solution.py:232
  5.7 0.0 copy-done.10
  5.7 0.2 convert_reduce_fusion.2
  5.9 0.1 select_reduce_fusion.3
  6.0 0.5 broadcast_add_fusion.2
  6.5 0.0 copy-done.8
  6.5 0.1 select_reduce_fusion.2
  6.6 0.0 copy-done.5
  6.6 0.6 convert_reduce_fusion.3
  7.2 0.7 convert_reduce_fusion.4
  7.9 0.0 copy-start.6
  7.9 0.5 copy-done.6
  8.5 0.7 convert_reduce_fusion.1
  9.2 0.7 sub.30
  9.9 0.0 copy-done.4
  9.9 0.0 copy-start.7
  9.9 0.0 copy-start.9
  9.9 0.0 copy-start.2
  9.9 1.3 %copy.13 = bf16[72,16,1024]{2,0,1:T(8,128)(2,1)S(1)} copy(bf16[72,16,1024]{2,1,0:T(8,128)(2,1)S(1)} %bitcast.14) | data formatting | bytes 4718592 | tf_op jit(solution)/shard_map/reshape | solution.py:323
  11.2 0.1 convert_reduce_fusion
  11.4 0.0 copy-done.7
  11.4 0.0 copy-done.9
  11.4 0.5 select_reduce_fusion
  11.9 0.0 collective-permute-done.1.fast_ref
  11.9 0.0 copy-done.2
  12.0 0.0 copy-start
  12.0 5.8 %copy-done = bf16[512,128,128]{2,1,0:T(8,128)(2,1)S(1)} copy-done((bf16[512,128,128]{2,1,0:T(8,128)(2,1)S(1)}, bf16[512,128,128]{2,1,0:T(8,128)(2,1)}, u32[]{:S(2)}) %copy-start) | copy-done | bytes 16777240
  17.7 8.0 %near_tiles.1.acc_in_ref = f32[33,72,128]{2,1,0:T(8,128)S(1)} custom-call(s32[512]{0:T(512)S(1)} %get-tuple-element.14.order_ref, s32[1]{0:T(128)} %bitcast.2.count_ref, bf16[512,128,128]{2,1,0:T(8,128)(2,1)S(1)} %copy-done, bf16[72,8192]{1,0:T(8,128)(2,1)S(1)} %copy-done.2, bf16[72,4096]{1,0:T(8,128)(2,1)S(1)} %collective-permute-done.1.fast_ref), custom_call_target="tpu_custom_call" | custom-call | flops 1207959552 | bytes 16777216 | tf_op jit(solution)/shard_map/near_tiles/pallas_call | solution.py:285
  25.7 0.0 collective-permute-done.slow_ref
  25.7 0.0 copy-start.1
  25.7 5.8 %copy-done.1 = bf16[512,128,128]{2,1,0:T(8,128)(2,1)S(1)} copy-done((bf16[512,128,128]{2,1,0:T(8,128)(2,1)S(1)}, bf16[512,128,128]{2,1,0:T(8,128)(2,1)}, u32[]{:S(2)}) %copy-start.1) | copy-done | bytes 16777240
  31.5 0.0 copy-start.3
  31.5 4.9 %far_tiles.1 = bf16[32,72,128]{2,1,0:T(8,128)(2,1)S(1)} custom-call(s32[512]{0:T(512)S(1)} %get-tuple-element.15.order_ref, s32[1]{0:T(128)} %bitcast.1.count_ref, bf16[512,128,128]{2,1,0:T(8,128)(2,1)S(1)} %copy-done.1, bf16[72,4096]{1,0:T(8,128)(2,1)S(1)} %collective-permute-done.slow_ref, f32[33,72,128]{2,1,0:T(8,128)S(1)} %near_tiles.1.acc_in_ref), custom_call_target="tpu_custom_call" | custom-call | flops 603979776 | bytes 8388608 | tf_op jit(solution)/shard_map/far_tiles/pallas_call | solution.py:303
  36.4 0.1 broadcast_in_dim.48.label_ref
  36.4 0.0 copy-done.3
  36.5 47.5 %exchange.1 = (bf16[4,72,128]{2,1,0:T(8,128)(2,1)S(1)}, bf16[32,1024]{1,0:T(8,128)(2,1)S(1)}) custom-call(bf16[16,2,72,128]{3,2,1,0:T(8,128)(2,1)S(1)} %bitcast.12, f32[16,8,128]{2,1,0:T(8,128)S(1)} %broadcast_in_dim.48.label_ref, bf16[16,72,1024]{2,1,0:T(8,128)(2,1)S(1)} %bitcast.11, f32[1,1024]{1,0:T(1,128)S(1)} %bitcast.13), custom_call_target="tpu_custom_call" | custom-call | tf_op jit(solution)/shard_map/exchange/pallas_call | solution.py:325
  84.0 0.6 copy.17
  84.6 0.6 copy.18
  (4 shorter events, 0.0 us)
Async XLA Ops:
  0.6 5.0 %copy-start.10 = (s32[16]{0:T(128)S(1)}, s32[16]{0:T(128)}, u32[]{:S(2)}) copy-start(s32[16]{0:T(128)} %param.13) | copy-start | bytes 196
  0.6 5.9 %copy-start.8 = (s32[512]{0:T(512)S(1)}, s32[512]{0:T(512)}, u32[]{:S(2)}) copy-start(s32[512]{0:T(512)} %param.11) | copy-start | bytes 6148
  0.7 5.9 %copy-start.5 = (s32[512]{0:T(512)S(1)}, s32[512]{0:T(512)}, u32[]{:S(2)}) copy-start(s32[512]{0:T(512)} %param.10) | copy-start | bytes 6148
  0.7 9.2 %copy-start.4 = (bf16[1152,1024]{1,0:T(8,128)(2,1)S(1)}, bf16[1152,1024]{1,0:T(8,128)(2,1)}, u32[]{:S(2)}) copy-start(bf16[1152,1024]{1,0:T(8,128)(2,1)} %param.14) | copy-start | bytes 7077892
  3.2 8.7 %collective-permute-start.1 = (bf16[72,4096]{1,0:T(8,128)(2,1)}, bf16[72,4096]{1,0:T(8,128)(2,1)S(1)}, u32[]{:S(2)}, u32[]{:S(2)}) collective-permute-start(bf16[72,4096]{1,0:T(8,128)(2,1)} %get-tuple-element.9), channel_id=1, source_target_pairs={{0,1},{1,0},{2,3},{3,2},{4,5},{5,4},{6,7},{7,6},{8,9},{9,8},{10,11... | collective-permute-start | bytes 1769480 | tf_op jit(solution)/shard_map/ppermute | solution.py:231
  3.9 21.9 %collective-permute-start = (bf16[72,4096]{1,0:T(8,128)(2,1)}, bf16[72,4096]{1,0:T(8,128)(2,1)S(1)}, u32[]{:S(2)}, u32[]{:S(2)}) collective-permute-start(bf16[72,4096]{1,0:T(8,128)(2,1)} %get-tuple-element.10), channel_id=1, source_target_pairs={{0,15},{1,2},{2,1},{3,4},{4,3},{5,6},{6,5},{7,8},{8,7},{9,10},{10,... | collective-permute-start | bytes 1769480 | tf_op jit(solution)/shard_map/ppermute | solution.py:232
  7.9 0.5 copy-start.6
  9.9 1.5 %copy-start.7 = (pred[512]{0:T(512)(128)(4,1)S(1)}, pred[512]{0:T(512)(128)(4,1)}, u32[]{:S(2)}) copy-start(pred[512]{0:T(512)(128)(4,1)} %copy-done.6) | copy-start | bytes 1540
  9.9 1.5 %copy-start.9 = (s32[512]{0:T(512)S(1)}, s32[512]{0:T(512)}, u32[]{:S(2)}) copy-start(s32[512]{0:T(512)} %convert_reduce_fusion.1) | copy-start | bytes 6148
  9.9 2.0 %copy-start.2 = (bf16[72,8192]{1,0:T(8,128)(2,1)S(1)}, bf16[72,8192]{1,0:T(8,128)(2,1)}, u32[]{:S(2)}) copy-start(bf16[72,8192]{1,0:T(8,128)(2,1)} %own_ref.1) | copy-start | bytes 3538948
  12.0 5.8 %copy-start = (bf16[512,128,128]{2,1,0:T(8,128)(2,1)S(1)}, bf16[512,128,128]{2,1,0:T(8,128)(2,1)}, u32[]{:S(2)}) copy-start(bf16[512,128,128]{2,1,0:T(8,128)(2,1)} %weight_ref.3) | copy-start | bytes 50331652
  25.7 5.8 %copy-start.1 = (bf16[512,128,128]{2,1,0:T(8,128)(2,1)S(1)}, bf16[512,128,128]{2,1,0:T(8,128)(2,1)}, u32[]{:S(2)}) copy-start(bf16[512,128,128]{2,1,0:T(8,128)(2,1)} %weight_ref.3) | copy-start | bytes 50331652
  31.5 4.9 %copy-start.3 = (f32[1024]{0:T(1024)S(1)}, f32[1024]{0:T(1024)}, u32[]{:S(2)}) copy-start(f32[1024]{0:T(1024)} %param.15) | copy-start | bytes 12292

commit v2 on v1

--- a/solution.py
+++ b/solution.py
@@ -10,80 +10,66 @@
 PATCH = 4
 CAP = 2
 TB_DEV = 4
-GROUP = 16
-DEPTH = 4
-
-
-def tile_steps(order_ref, count_ref, weight_ref, cells_ref, acc_ref, buffer, sems):
-    groups = (count_ref[0] + GROUP - 1) // GROUP
-
-    def fetch(group):
-        slot = lax.rem(group, DEPTH)
-        for i in range(GROUP):
-            tile = order_ref[group * GROUP + i] & 0xFFF
-            pltpu.make_async_copy(
-                weight_ref.at[tile], buffer.at[slot, i], sems.at[slot]
-            ).start()
-
-    for group in range(DEPTH):
-        @pl.when(group < groups)
-        def _():
-            fetch(group)
-
-    def step(group, _):
-        slot = lax.rem(group, DEPTH)
-        pltpu.make_async_copy(
-            weight_ref.at[pl.ds(0, GROUP)], buffer.at[slot], sems.at[slot]
-        ).wait()
-        for first in range(0, GROUP, 4):
-            rows, products = [], []
-            for i in range(first, first + 4):
-                code = order_ref[group * GROUP + i]
-                block = (code >> 12) & 0xFF
-                rows.append(code >> 20)
-                cells = cells_ref[:, pl.ds(pl.multiple_of(block * 128, 128), 128)]
-                products.append(
-                    jnp.dot(cells, buffer[slot, i], preferred_element_type=jnp.float32)
-                )
-            for row, product in zip(rows, products):
-                acc_ref[row] += product
-
-        @pl.when(group + DEPTH < groups)
-        def _():
-            fetch(group + DEPTH)
-
-        return 0
-
-    lax.fori_loop(0, groups, step, 0)
-
-
-def near_kernel(
-    order_ref, count_ref, weight_ref, own_ref, fast_ref, acc_ref, cells, buffer, sems, cell_sem
-):
-    own_cells = own_ref.shape[1]
-    copies = [
-        pltpu.make_async_copy(own_ref, cells.at[:, pl.ds(0, own_cells)], cell_sem.at[0]),
-        pltpu.make_async_copy(
-            fast_ref, cells.at[:, pl.ds(own_cells, fast_ref.shape[1])], cell_sem.at[1]
-        ),
-    ]
-    for copy in copies:
-        copy.start()
-    acc_ref[...] = jnp.zeros_like(acc_ref)
-    for copy in copies:
-        copy.wait()
-    tile_steps(order_ref, count_ref, weight_ref, cells, acc_ref, buffer, sems)
-
-
-def far_kernel(
-    order_ref, count_ref, weight_ref, slow_ref, acc_in_ref, out_ref, acc, buffer, sems, acc_sem
-):
-    copy = pltpu.make_async_copy(acc_in_ref, acc, acc_sem)
+QUAD = 4
+UNROLL = 4
+
+
+def load_kernel(after_ref, weight_ref, held_ref, sem):
+    copy = pltpu.make_async_copy(weight_ref, held_ref, sem)
     copy.start()
     copy.wait()
-    tile_steps(order_ref, count_ref, weight_ref, slow_ref, acc, buffer, sems)
-    rows = out_ref.shape[0]
-    out_ref[...] = acc[pl.ds(0, rows)].astype(jnp.bfloat16)
+
+
+def tiles_kernel(order_ref, count_ref, weight_ref, own_ref, fast_ref, slow_ref, out_ref, cells, acc):
+    own_blocks = own_ref.shape[1] // 128
+    rim_blocks = fast_ref.shape[1] // 128
+
+    def fill(ref, first, blocks):
+        def step(i, _):
+            for j in range(4):
+                b = i * 4 + j
+                cells[first + b] = ref[:, pl.ds(pl.multiple_of(b * 128, 128), 128)]
+            return 0
+
+        lax.fori_loop(0, blocks // 4, step, 0)
+
+    fill(own_ref, 0, own_blocks)
+    fill(fast_ref, own_blocks, rim_blocks)
+    fill(slow_ref, own_blocks + rim_blocks, rim_blocks)
+    last = cells.shape[0] - 1
+    cells[last] = jnp.zeros(cells.shape[1:], cells.dtype)
+    acc[...] = jnp.zeros_like(acc)
+
+    def step(group, _):
+        rows, products = [], []
+        for u in range(UNROLL):
+            xs, ws = [], []
+            for i in range(QUAD):
+                code = order_ref[(group * UNROLL + u) * QUAD + i]
+                if i == 0:
+                    rows.append(code >> 20)
+                xs.append(cells[(code >> 12) & 0xFF])
+                ws.append(weight_ref[code & 0xFFF])
+            products.append(
+                jnp.dot(
+                    jnp.concatenate(xs, axis=1),
+                    jnp.concatenate(ws, axis=0),
+                    preferred_element_type=jnp.float32,
+                )
+            )
+        for row, product in zip(rows, products):
+            acc[row] += product
+        return 0
+
+    lax.fori_loop(0, count_ref[0], step, 0)
+    peers = out_ref.shape[0]
+
+    def store(p, _):
+        for r in range(CAP):
+            out_ref[p, r] = acc[p * CAP + r].astype(jnp.bfloat16)
+        return 0
+
+    lax.fori_loop(0, peers, store, 0)
 
 
 def exchange_kernel(
@@ -217,6 +203,7 @@
     own_blocks = own_cells // block_size
     rim_blocks = own_blocks // 2
     rim = rim_blocks * block_size
+    ext_blocks = own_blocks + 2 * rim_blocks
     tile_total = tile_weight.shape[0]
     slot_total = dest_block.shape[0]
     emb = embed_weight.shape[1]
@@ -244,53 +231,58 @@
     ).astype(jnp.float32)
 
     tile_ids = jnp.arange(tile_total, dtype=jnp.int32)
-    row_of = jnp.sum(
-        jnp.where(tile_slot[:, None] == slot_ids[None, :], position[None, :], 0), axis=1
-    )
     live = tile_ids < tile_count[0]
-    left = tile_source < rim_blocks
-    right = tile_source >= rim_blocks + own_blocks
-    is_far = jnp.where(odd == 1, right, left)
-    near = live & ~is_far
-    far = live & is_far
-    near_block = jnp.where(
-        left,
-        tile_source + own_blocks,
-        jnp.where(right, tile_source - rim_blocks, tile_source - rim_blocks),
-    )
-    far_block = jnp.where(left, tile_source, tile_source - rim_blocks - own_blocks)
-    block = jnp.where(is_far, far_block, near_block)
-    code = tile_ids | (block << 12) | (row_of << 20)
-    pad_code = rows_out << 20
-
-    def listed(chosen):
-        rank = jnp.sum(
-            (chosen[None, :] & (tile_ids[None, :] < tile_ids[:, None])).astype(jnp.int32), axis=1
-        )
-        hit = chosen[None, :] & (rank[None, :] == tile_ids[:, None])
-        order = jnp.sum(jnp.where(hit, code[None, :] - pad_code, 0), axis=1) + pad_code
-        return order, jnp.sum(chosen.astype(jnp.int32)).reshape(1)
-
-    near_order, near_count = listed(near)
-    far_order, far_count = listed(far)
+    key = jnp.where(live, tile_slot, slot_total)
+    rank = jnp.sum(
+        ((key[None, :] == key[:, None]) & (tile_ids[None, :] < tile_ids[:, None])).astype(jnp.int32),
+        axis=1,
+    )
+    held = jnp.sum((key[None, :] == slot_ids[:, None]).astype(jnp.int32), axis=1)
+    quads = (held + QUAD - 1) // QUAD
+    base = jnp.sum(jnp.where(slot_ids[None, :] < slot_ids[:, None], quads[None, :], 0), axis=1) * QUAD
+    list_total = -(-(tile_total + (QUAD - 1) * slot_total) // (QUAD * UNROLL)) * QUAD * UNROLL
+    table = base + (position << 12)
+    entry = jnp.sum(jnp.where(key[:, None] == slot_ids[None, :], table[None, :], 0), axis=1)
+    place = jnp.where(live, (entry & 0xFFF) + rank, -1)
+    block = jnp.where(
+        tile_source < rim_blocks,
+        tile_source + own_blocks + jnp.where(odd == 1, 0, rim_blocks),
+        tile_source
+        - rim_blocks
+        + jnp.where((tile_source >= rim_blocks + own_blocks) & (odd == 1), rim_blocks, 0),
+    )
+    code = tile_ids | (block << 12) | ((entry >> 12) << 20)
+    pad_code = (rows_out << 20) | (ext_blocks << 12)
+    spots = jnp.arange(list_total, dtype=jnp.int32)
+    order = (
+        jnp.sum(jnp.where(place[None, :] == spots[:, None], code[None, :] - pad_code, 0), axis=1)
+        + pad_code
+    )
+    steps = ((jnp.sum(quads) + UNROLL - 1) // UNROLL).reshape(1)
 
     smem = pl.BlockSpec(memory_space=pltpu.SMEM)
     vmem = pl.BlockSpec(memory_space=pltpu.VMEM)
     hbm = pl.BlockSpec(memory_space=pl.ANY)
-    acc_shape = (rows_out + 1, channels, block_size)
-    ring = [
-        pltpu.VMEM((DEPTH, GROUP, block_size, block_size), jnp.bfloat16),
-        pltpu.SemaphoreType.DMA((DEPTH,)),
-    ]
-    partial = pl.pallas_call(
-        near_kernel,
-        out_shape=jax.ShapeDtypeStruct(acc_shape, jnp.float32),
-        in_specs=[smem, smem, hbm, hbm, hbm],
+    weight_held = pl.pallas_call(
+        load_kernel,
+        out_shape=jax.ShapeDtypeStruct(tile_weight.shape, tile_weight.dtype),
+        in_specs=[smem, hbm],
+        out_specs=vmem,
+        scratch_shapes=[pltpu.SemaphoreType.DMA],
+        compiler_params=pltpu.CompilerParams(vmem_limit_bytes=24 * 2**20),
+        cost_estimate=pl.CostEstimate(
+            flops=0, bytes_accessed=tile_weight.size * 2, transcendentals=0
+        ),
+        name="load",
+    )(held, tile_weight)
+    outgoing = pl.pallas_call(
+        tiles_kernel,
+        out_shape=jax.ShapeDtypeStruct((peers, CAP, channels, block_size), jnp.bfloat16),
+        in_specs=[smem, smem, vmem, vmem, vmem, vmem],
         out_specs=vmem,
         scratch_shapes=[
-            pltpu.VMEM((channels, own_cells + rim), jnp.bfloat16),
-            *ring,
-            pltpu.SemaphoreType.DMA((2,)),
+            pltpu.VMEM((ext_blocks + 1, channels, block_size), jnp.bfloat16),
+            pltpu.VMEM((rows_out + 1, channels, block_size), jnp.float32),
         ],
         compiler_params=pltpu.CompilerParams(vmem_limit_bytes=32 * 2**20),
         cost_estimate=pl.CostEstimate(
@@ -298,26 +290,8 @@
             bytes_accessed=tile_weight.size * 2,
             transcendentals=0,
         ),
-        name="near_tiles",
-    )(near_order, near_count, tile_weight, source, fast)
-    outgoing = pl.pallas_call(
-        far_kernel,
-        out_shape=jax.ShapeDtypeStruct((rows_out, channels, block_size), jnp.bfloat16),
-        in_specs=[smem, smem, hbm, vmem, hbm],
-        out_specs=vmem,
-        scratch_shapes=[
-            pltpu.VMEM(acc_shape, jnp.float32),
-            *ring,
-            pltpu.SemaphoreType.DMA,
-        ],
-        compiler_params=pltpu.CompilerParams(vmem_limit_bytes=32 * 2**20),
-        cost_estimate=pl.CostEstimate(
-            flops=tile_total * channels * block_size**2,
-            bytes_accessed=tile_weight.size,
-            transcendentals=0,
-        ),
-        name="far_tiles",
-    )(far_order, far_count, tile_weight, slow, partial)
+        name="tiles",
+    )(order, steps, weight_held, source, fast, slow)
 
     per_patch = PATCH * PATCH
     embed_turned = embed_weight.reshape(channels, per_patch, emb).transpose(1, 0, 2)
@@ -347,7 +321,7 @@
         ),
         name="exchange",
     )(
-        outgoing.reshape(peers, CAP, channels, block_size),
+        outgoing,
         names,
         embed_turned,
         embed_bias.reshape(1, emb),

time: 84.5 us -> 60.6 us (0.72)
  Pallas kernels: 60.4 us -> 38.6 us
  local copies, waits for them, and re-layouts: 17.9 us -> 16.6 us
  other arithmetic: 3.64 us -> 2.43 us
    pallas_call x1, Pallas kernels: 47.5 us -> 27.4 us  [local(): pl.pallas_call(functools.partial(exchange_kernel, peers), out_shape=(jax....]
    reduce_sum x6 -> x5, other arithmetic: 2.81 us -> 0.78 us  [the longest x1 0.25 us: local(): jnp.sum(((key[None, :] == key[:, None]) & (tile_ids[None, :] < tile_ids[:...]
    pallas_call x2, Pallas kernels: 12.8 us -> 11.1 us  [the longest x1 6.48 us: local(): pl.pallas_call(load_kernel, out_shape=jax.ShapeDtypeStruct(tile_weight.sh...]
    unnamed x24 -> x16, local copies, waits for them, and re-layouts: 13.4 us -> 12.8 us
  transfers between devices with their start and end apart: 2 -> 2, of which waited for: 0 -> 0; matrix products, arithmetic and copies ran while one was open for 7% -> 6% of each run, Pallas kernels for 9% -> 11%
where the time goes in v2:
time: 60.6 us; the launch traced here: 61.5 us
  Pallas kernels  38.6 us (64%)
  local copies, waits for them, and re-layouts  16.6 us (27%)
  other arithmetic  2.43 us (4%)
  between operations  2.13 us (4%)
  starting transfers between devices  1.8 us (3%)
    pallas_call x1, Pallas kernels, local(): pl.pallas_call(functools.partial(exchange_kernel, peers), out_shape=(jax....  27.4 us
    unnamed x16, local copies, waits for them, and re-layouts  12.8 us
    pallas_call x1, Pallas kernels, local(): pl.pallas_call(load_kernel, out_shape=jax.ShapeDtypeStruct(tile_weight.sh...  6.48 us
    pallas_call x1, Pallas kernels, local(): pl.pallas_call(tiles_kernel, out_shape=jax.ShapeDtypeStruct((peers, CAP,...  4.66 us
    dynamic_slice x1, local copies, waits for them, and re-layouts, local(): lax.dynamic_slice_in_dim(source, jnp.where(odd == 1, tail_start, head_sta...  2.4 us
    reshape x1, local copies, waits for them, and re-layouts, local(): embed_weight.reshape(channels, per_patch, emb).transpose(1, 0, 2)  1.3 us
  transfers between devices with their start and end apart: 2, of which 0 were waited for; matrix products, arithmetic and copies ran while one was open for 6% of the time, Pallas kernels for 11%

profile of v2, /device:TPU:15, one launch (start us, length us, event | category | flops | bytes accessed | tf_op | source)
XLA Modules:
  0.0 61.5 jit_solution(9259783001729041143)
XLA Ops:
  0.6 0.0 copy-start.5
  0.7 0.0 copy-start.6
  0.7 2.4 %constant_dynamic-slice_fusion.1 = (bf16[72,4096]{1,0:T(8,128)(2,1)}, bf16[72,4096]{1,0:T(8,128)(2,1)}) fusion(bf16[72,8192]{1,0:T(8,128)(2,1)} %own_ref.1, s32[]{:T(128)S(6)} %select_n.90, s32[]{:T(128)S(6)} %select_n.89), kind=kLoop, calls=%fused_computation.35 | loop fusion | bytes 2359304 | tf_op jit(solution)/shard_map/dynamic_slice | solution.py:214
  3.1 0.7 %collective-permute-start = (bf16[72,4096]{1,0:T(8,128)(2,1)}, bf16[72,4096]{1,0:T(8,128)(2,1)}, u32[]{:S(2)}, u32[]{:S(2)}) collective-permute-start(bf16[72,4096]{1,0:T(8,128)(2,1)} %get-tuple-element.7), channel_id=1, source_target_pairs={{0,1},{1,0},{2,3},{3,2},{4,5},{5,4},{6,7},{7,6},{8,9},{9,8},{10,11... | collective-permute-start | bytes 1769480 | tf_op jit(solution)/shard_map/ppermute | solution.py:218
  3.7 1.1 %collective-permute-start.1 = (bf16[72,4096]{1,0:T(8,128)(2,1)}, bf16[72,4096]{1,0:T(8,128)(2,1)}, u32[]{:S(2)}, u32[]{:S(2)}) collective-permute-start(bf16[72,4096]{1,0:T(8,128)(2,1)} %get-tuple-element.6), channel_id=1, source_target_pairs={{0,15},{1,2},{2,1},{3,4},{4,3},{5,6},{6,5},{7,8},{8,7},{9,10},{10,... | collective-permute-start | bytes 1769480 | tf_op jit(solution)/shard_map/ppermute | solution.py:219
  5.5 0.0 copy-done.5
  5.5 0.1 convert_reduce_fusion.1.after_ref
  5.7 0.2 convert_reduce_fusion
  5.9 0.0 copy-done.6
  5.9 0.6 %fusion.3 = (s32[16]{0:T(128)S(1)}, s32[16]{0:T(128)S(1)}, s32[]{:T(128)}, s32[16]{0:T(128)S(1)}) fusion(s32[16]{0:T(128)S(1)} %copy-done.6, s32[16]{0:T(128)S(1)} %convert_reduce_fusion.1.after_ref), kind=kLoop, calls=%fused_computation.31 | loop fusion | flops 591 | bytes 324 | tf_op jit(solution)/shard_map/add | solution.py:227
  6.6 0.2 convert_reduce_fusion.2
  6.7 0.1 select_reduce_fusion.3
  6.9 0.1 select_reduce_fusion.1
  7.0 0.1 select_reduce_fusion.2
  7.1 0.1 sub.41
  7.8 0.0 copy-start.4
  7.8 6.5 %load.1.weight_ref = bf16[512,128,128]{2,1,0:T(8,128)(2,1)S(1)} custom-call(s32[16]{0:T(128)S(1)} %convert_reduce_fusion.1.after_ref, bf16[512,128,128]{2,1,0:T(8,128)(2,1)} %weight_ref.1), custom_call_target="tpu_custom_call" | custom-call | bytes 16777216 | tf_op jit(solution)/shard_map/load/pallas_call | solution.py:266
  14.3 0.0 copy-start
  14.3 5.7 %copy-done = bf16[512,128,128]{2,1,0:T(8,128)(2,1)} copy-done((bf16[512,128,128]{2,1,0:T(8,128)(2,1)}, bf16[512,128,128]{2,1,0:T(8,128)(2,1)S(1)}, u32[]{:S(2)}) %copy-start) | copy-done | bytes 16777240
  20.1 0.0 copy-done.4
  20.1 0.0 copy-start.2
  20.1 1.3 %copy.13 = bf16[72,16,1024]{2,0,1:T(8,128)(2,1)S(1)} copy(bf16[72,16,1024]{2,1,0:T(8,128)(2,1)S(1)} %bitcast.11) | data formatting | bytes 4718592 | tf_op jit(solution)/shard_map/reshape | solution.py:297
  21.4 0.7 %add_select_fusion = (s32[512]{0:T(512)S(1)}, s32[512]{0:T(512)S(1)}) fusion(s32[512]{0:T(512)S(1)} %convert_reduce_fusion, s32[512]{0:T(512)S(1)} %select_reduce_fusion.1, s32[]{:T(128)} %bitcast.8, pred[]{:T(512)S(6)} %eq.103, s32[512]{0:T(512)} %param.10, s32[]{:T(128)S(6)} %select_n.84), kind=kLoop, calls=%fused_computation.19 | loop fusion | flops 9728 | bytes 10249 | tf_op jit(solution)/shard_map/jit(_where)/select_n | solution.py:246
  22.1 0.2 select_reduce_fusion
  22.3 0.0 collective-permute-done.fast_ref
  22.3 0.0 collective-permute-done.1.slow_ref
  22.3 0.0 copy-done.2
  22.3 0.0 copy-start.1
  22.3 5.8 %copy-done.1 = bf16[512,128,128]{2,1,0:T(8,128)(2,1)S(1)} copy-done((bf16[512,128,128]{2,1,0:T(8,128)(2,1)S(1)}, bf16[512,128,128]{2,1,0:T(8,128)(2,1)}, u32[]{:S(2)}) %copy-start.1) | copy-done | bytes 16777240
  28.1 0.0 copy-start.3
  28.1 4.7 %tiles.1.out_ref = bf16[16,2,72,128]{3,2,1,0:T(8,128)(2,1)S(1)} custom-call(s32[560]{0:T(1024)S(1)} %broadcast_add_fusion.order_ref, s32[1]{0:T(128)} %bitcast.1.count_ref, bf16[512,128,128]{2,1,0:T(8,128)(2,1)S(1)} %copy-done.1, bf16[72,8192]{1,0:T(8,128)(2,1)S(1)} %copy-done.2, bf16[72,4096]{1,0:T(8,128)(2,1)} %collective-permute-done.fast_ref, ...), custom_call_target="tpu_custom_call" | custom-call | flops 1207959552 | bytes 16777216 | tf_op jit(solution)/shard_map/tiles/pallas_call | solution.py:278
  32.8 0.1 broadcast_in_dim.100.label_ref
  32.8 0.0 copy-done.3
  32.8 27.4 %exchange.1 = (bf16[4,72,128]{2,1,0:T(8,128)(2,1)S(1)}, bf16[32,1024]{1,0:T(8,128)(2,1)S(1)}) custom-call(bf16[16,2,72,128]{3,2,1,0:T(8,128)(2,1)S(1)} %tiles.1.out_ref, f32[16,8,128]{2,1,0:T(8,128)S(1)} %broadcast_in_dim.100.label_ref, bf16[16,72,1024]{2,1,0:T(8,128)(2,1)S(1)} %bitcast.9, f32[1,1024]{1,0:T(1,128)S(1)} %bitcast.10), custom_call_target="tpu_custom_call" | custom-call | tf_op jit(solution)/shard_map/exchange/pallas_call | solution.py:299
  60.3 0.6 %copy.17 = bf16[4,72,128]{2,1,0:T(8,128)(2,1)} copy(bf16[4,72,128]{2,1,0:T(8,128)(2,1)S(1)} %get-tuple-element.16) | data formatting | bytes 147456
  60.9 0.6 %copy.18 = bf16[32,1024]{1,0:T(8,128)(2,1)} copy(bf16[32,1024]{1,0:T(8,128)(2,1)S(1)} %get-tuple-element.17) | data formatting | bytes 131072
  (5 shorter events, 0.0 us)
Async XLA Ops:
  0.6 4.9 %copy-start.5 = (s32[512]{0:T(512)S(1)}, s32[512]{0:T(512)}, u32[]{:S(2)}) copy-start(s32[512]{0:T(512)} %param.11) | copy-start | bytes 6148
  0.7 5.3 %copy-start.6 = (s32[16]{0:T(128)S(1)}, s32[16]{0:T(128)}, u32[]{:S(2)}) copy-start(s32[16]{0:T(128)} %param.13) | copy-start | bytes 196
  3.1 19.2 %collective-permute-start = (bf16[72,4096]{1,0:T(8,128)(2,1)}, bf16[72,4096]{1,0:T(8,128)(2,1)}, u32[]{:S(2)}, u32[]{:S(2)}) collective-permute-start(bf16[72,4096]{1,0:T(8,128)(2,1)} %get-tuple-element.7), channel_id=1, source_target_pairs={{0,1},{1,0},{2,3},{3,2},{4,5},{5,4},{6,7},{7,6},{8,9},{9,8},{10,11... | collective-permute-start | bytes 1769480 | tf_op jit(solution)/shard_map/ppermute | solution.py:218
  3.7 18.6 %collective-permute-start.1 = (bf16[72,4096]{1,0:T(8,128)(2,1)}, bf16[72,4096]{1,0:T(8,128)(2,1)}, u32[]{:S(2)}, u32[]{:S(2)}) collective-permute-start(bf16[72,4096]{1,0:T(8,128)(2,1)} %get-tuple-element.6), channel_id=1, source_target_pairs={{0,15},{1,2},{2,1},{3,4},{4,3},{5,6},{6,5},{7,8},{8,7},{9,10},{10,... | collective-permute-start | bytes 1769480 | tf_op jit(solution)/shard_map/ppermute | solution.py:219
  7.8 12.2 %copy-start.4 = (bf16[1152,1024]{1,0:T(8,128)(2,1)S(1)}, bf16[1152,1024]{1,0:T(8,128)(2,1)}, u32[]{:S(2)}) copy-start(bf16[1152,1024]{1,0:T(8,128)(2,1)} %param.14) | copy-start | bytes 7077892
  14.3 5.7 %copy-start = (bf16[512,128,128]{2,1,0:T(8,128)(2,1)}, bf16[512,128,128]{2,1,0:T(8,128)(2,1)S(1)}, u32[]{:S(2)}) copy-start(bf16[512,128,128]{2,1,0:T(8,128)(2,1)S(1)} %load.1.weight_ref) | copy-start | bytes 50331652
  20.1 2.3 %copy-start.2 = (bf16[72,8192]{1,0:T(8,128)(2,1)S(1)}, bf16[72,8192]{1,0:T(8,128)(2,1)}, u32[]{:S(2)}) copy-start(bf16[72,8192]{1,0:T(8,128)(2,1)} %own_ref.1) | copy-start | bytes 3538948
  22.3 5.8 %copy-start.1 = (bf16[512,128,128]{2,1,0:T(8,128)(2,1)S(1)}, bf16[512,128,128]{2,1,0:T(8,128)(2,1)}, u32[]{:S(2)}) copy-start(bf16[512,128,128]{2,1,0:T(8,128)(2,1)} %copy-done) | copy-start | bytes 50331652
  28.1 4.8 %copy-start.3 = (f32[1024]{0:T(1024)S(1)}, f32[1024]{0:T(1024)}, u32[]{:S(2)}) copy-start(f32[1024]{0:T(1024)} %param.15) | copy-start | bytes 12292
